TPU v7x, 256 devices: a whole 4x4x8 slice. The times are simulated.
256 devices in a mesh: blk: 32 (over z, x_lo, core), head: 8 (over x_hi, y).
Axes of the slice: x: 4 (x_hi: 2, x_lo: 2; x = x_hi * 2 + x_lo), y: 4, z: 8, core: 2. Of those that a mesh axis runs over, the one named last changes fastest.
Arguments:
- query_tokens: bfloat16 [16384, 3072], P(('blk', 'head')), may hold values from -12 to 12
- key_tokens: bfloat16 [16384, 3072], P(('blk', 'head')), may hold values from -6 to 6
- value_tokens: bfloat16 [16384, 3072], P(('blk', 'head')), may hold values from -6 to 6
- out_weight: bfloat16 [3072, 3072], P('head'), may hold values from -1.75 to 1.75
- kv_blocks: int32 [128, 16], P('blk'), may hold values from -1 to 127, as said below
Outputs:
- projected: bfloat16 [16384, 3072], P(('blk', 'head'))
Inputs may be any that keep to these rules, and one draw needn't show every extreme that they name: `kv_blocks`: row i lists the key blocks of 128 tokens that query block i attends to; let G = floor(i / 4). Entry 0 is i. Entry 1 is one of the blocks 4 * M to 4 * M + 3 with M = (G + 16) mod 32. Entry j >= 2 is -1 (absent) or one of the blocks 4 * (G + o) to 4 * (G + o) + 3, with o = j // 2 for even j and o = -(j - 1) // 2 for odd j; it is present whenever j < 8 and those blocks exist. Entries of one row are distinct.
All inputs are finite; a program needn't handle non-finite values.
Results may differ from a plain program's by a relative error of at most 0.012.
Values may be sent and summed in bfloat16 or wider, within the bound.
A program may use at most 128 MiB of HBM per device.

v0:
```python
import math
import jax
import jax.numpy as jnp
from jax import lax
from jax.sharding import PartitionSpec as P

HD = 128
masked_low = -1e30


def sparse_attend(query_sets, key_sets, value_sets, present):
    blocks_dev = present.shape[0]
    slots = present.shape[1]
    block_rows = query_sets.shape[2]
    scaling = 1.0 / math.sqrt(HD)
    allowed = jnp.broadcast_to(present[:, :, None], (blocks_dev, slots, block_rows)).reshape(
        blocks_dev, slots * block_rows
    )
    scores = (
        jnp.einsum("hbqd,hbkd->hbqk", query_sets, key_sets, preferred_element_type=jnp.float32)
        * scaling
    )
    mask_full = allowed[None, :, None, :]
    peak_value = jnp.max(jnp.where(mask_full, scores, masked_low), axis=-1, keepdims=True)
    weights = jnp.where(mask_full, jnp.exp(scores - peak_value), 0.0)
    denom = jnp.sum(weights, axis=-1)
    outputs = jnp.einsum(
        "hbqk,hbkd->hbqd",
        weights.astype(jnp.bfloat16),
        value_sets,
        preferred_element_type=jnp.float32,
    )
    return outputs / denom[..., None]


def on_device(query_tokens, key_tokens, value_tokens, out_weight, kv_blocks):
    queries, key_rows, value_rows = (
        lax.all_to_all(query_tokens, "head", split_axis=1, concat_axis=0, tiled=True),
        lax.all_to_all(key_tokens, "head", split_axis=1, concat_axis=0, tiled=True),
        lax.all_to_all(value_tokens, "head", split_axis=1, concat_axis=0, tiled=True),
    )
    row_total = queries.shape[0]
    feature_width = queries.shape[1]
    heads_dev = feature_width // HD
    blocks_dev = kv_blocks.shape[0]
    block_rows = row_total // blocks_dev
    slots = kv_blocks.shape[1]
    query_heads = queries.reshape(row_total, heads_dev, HD).transpose(1, 0, 2)
    query_sets = query_heads.reshape(heads_dev, blocks_dev, block_rows, HD)
    key_heads = key_rows.reshape(row_total, heads_dev, HD).transpose(1, 0, 2)
    value_heads = value_rows.reshape(row_total, heads_dev, HD).transpose(1, 0, 2)
    present = kv_blocks >= 0
    safe_index = jnp.maximum(kv_blocks, 0)
    gathered_keys, gathered_values = (
        lax.all_gather(key_heads, "blk", axis=1, tiled=True),
        lax.all_gather(value_heads, "blk", axis=1, tiled=True),
    )
    total_blocks = gathered_keys.shape[1] // block_rows
    source_keys = gathered_keys.reshape(heads_dev, total_blocks, block_rows, HD)
    source_values = gathered_values.reshape(heads_dev, total_blocks, block_rows, HD)
    flat_index = safe_index.reshape(blocks_dev * slots)
    key_sets = jnp.take(source_keys, flat_index, axis=1).reshape(
        heads_dev, blocks_dev, slots * block_rows, HD
    )
    value_sets = jnp.take(source_values, flat_index, axis=1).reshape(
        heads_dev, blocks_dev, slots * block_rows, HD
    )
    outputs = sparse_attend(query_sets, key_sets, value_sets, present)
    attended = (
        outputs.reshape(heads_dev, row_total, HD)
        .transpose(1, 0, 2)
        .reshape(row_total, feature_width)
    )
    attended = attended.astype(jnp.bfloat16)
    return lax.psum_scatter(
        jnp.dot(attended, out_weight, preferred_element_type=jnp.float32).astype(jnp.bfloat16),
        "head",
        scatter_dimension=0,
        tiled=True,
    )


def solution(mesh):
    placed = (
        P(("blk", "head"), None),
        P(("blk", "head"), None),
        P(("blk", "head"), None),
        P("head", None),
        P("blk", None),
    )
    return jax.shard_map(
        on_device, mesh=mesh, in_specs=placed, out_specs=P(("blk", "head"), None), check_vma=False
    )
```

profile of v0, /device:TPU:32, one launch (start us, length us, event | category | flops | bytes accessed | tf_op | source)
XLA Modules:
  0.0 322.1 jit_solution(16858350131159604797)
XLA Ops:
  6.5 1.2 copy.46
  7.7 16.9 %all_to_all.48 = bf16[64,8,384]{2,0,1:T(8,128)(2,1)S(1)} all-to-all(bf16[64,8,384]{2,0,1:T(8,128)(2,1)S(1)} %bitcast.64), channel_id=1, replica_groups=mesh['blk'=32,'head'=8] {'head'}, dimensions={1} | all-to-all | bytes 786432 | tf_op jit(solution)/shard_map/all_to_all | solution.py:39
  24.7 0.1 reshape.52
  24.8 0.8 copy.26
  25.6 1.0 copy.44
  26.7 12.0 %all_to_all.49 = bf16[64,8,384]{2,0,1:T(8,128)(2,1)S(1)} all-to-all(bf16[64,8,384]{2,0,1:T(8,128)(2,1)S(1)} %bitcast.65), channel_id=1, replica_groups=mesh['blk'=32,'head'=8] {'head'}, dimensions={1} | all-to-all | bytes 786432 | tf_op jit(solution)/shard_map/all_to_all | solution.py:40
  38.7 0.1 reshape.58
  38.8 0.8 copy.31
  39.7 1.9 copy.45
  41.5 3.5 %all-to-all-start.1 = ((bf16[64,8,384]{2,0,1:T(8,128)(2,1)}), bf16[64,8,384]{2,0,1:T(8,128)(2,1)S(1)}, u32[]{:S(2)}, u32[]{:S(2)}) async-start(bf16[64,8,384]{2,0,1:T(8,128)(2,1)} %bitcast.51), calls=%async_computation.1 | async-start | bytes 786432 | tf_op jit(solution)/shard_map/all_to_all | solution.py:38
  45.3 8.9 %all-to-all-done.1 = bf16[64,8,384]{2,0,1:T(8,128)(2,1)S(1)} async-done(((bf16[64,8,384]{2,0,1:T(8,128)(2,1)}), bf16[64,8,384]{2,0,1:T(8,128)(2,1)S(1)}, u32[]{:S(2)}, u32[]{:S(2)}) %all-to-all-start.1) | async-done | bytes 393248 | tf_op jit(solution)/shard_map/all_to_all | solution.py:38
  54.2 0.1 reshape.56
  54.4 51.7 %all-gather.3.cloned.1.call-done = bf16[3,16384,128]{2,1,0:T(8,128)(2,1)} async-done(((bf16[3,512,128]{2,1,0:T(8,128)(2,1)}), bf16[3,16384,128]{2,1,0:T(8,128)(2,1)}) %all-gather.3.cloned.1.call-update) | async-done | bytes 12582928 | tf_op jit(solution)/shard_map/all_gather | solution.py:55
  106.1 8.6 %gather_fusion = bf16[64,3,128,128]{3,2,1,0:T(8,128)(2,1)} fusion(bf16[3,128,128,128]{3,2,1,0:T(8,128)(2,1)} %bitcast.56, s32[1024]{0:T(1024)S(1)} %pad_clamp_fusion), kind=kCustom, calls=%fused_computation.clone | custom fusion | bytes 12583168 | tf_op jit(solution)/shard_map/jit(_take)/gather | solution.py:62
  114.7 72.9 %all-gather.5.cloned.1.call-done = bf16[3,16384,128]{2,1,0:T(8,128)(2,1)} async-done(((bf16[3,512,128]{2,1,0:T(8,128)(2,1)}), bf16[3,16384,128]{2,1,0:T(8,128)(2,1)}) %all-gather.5.cloned.1.call-update) | async-done | bytes 12582928 | tf_op jit(solution)/shard_map/all_gather | solution.py:56
  187.6 8.5 %gather_fusion.1 = bf16[64,3,128,128]{3,2,1,0:T(8,128)(2,1)} fusion(bf16[3,128,128,128]{3,2,1,0:T(8,128)(2,1)} %bitcast.57, s32[1024]{0:T(1024)S(1)} %pad_clamp_fusion), kind=kCustom, calls=%fused_computation.1.clone | custom fusion | bytes 12583168 | tf_op jit(solution)/shard_map/jit(_take)/gather | solution.py:65
  196.1 5.5 %select_bitcast_fusion.1 = (bf16[3,64,128,128]{3,2,0,1:T(8,128)(2,1)S(1)}, bf16[3,64,128,128]{3,2,0,1:T(8,128)(2,1)S(1)}) fusion(bf16[64,3,128,128]{3,2,1,0:T(8,128)(2,1)} %gather_fusion, pred[64]{0:T(512)(128)(4,1)S(1)} %compare_and_fusion, bf16[64,3,128,128]{3,2,1,0:T(8,128)(2,1)} %gather_fusion.1), kind=kLoop, calls=%fused_computation.11 | loop fusion | flops 6291456 | bytes 25165888 | tf_op jit(solution)/shard_map/jit(_take)/select_n | solution.py:62
  201.7 4.0 %copy.27 = bf16[3,64,128,128]{3,2,1,0:T(8,128)(2,1)} copy(bf16[3,64,128,128]{3,2,0,1:T(8,128)(2,1)S(1)} %get-tuple-element.6) | data formatting | bytes 12582912 | tf_op jit(solution)/shard_map/jit(_take)/select_n | solution.py:62
  205.7 4.0 %copy.32 = bf16[3,64,128,128]{3,2,1,0:T(8,128)(2,1)} copy(bf16[3,64,128,128]{3,2,0,1:T(8,128)(2,1)S(1)} %get-tuple-element.7) | data formatting | bytes 12582912 | tf_op jit(solution)/shard_map/jit(_take)/select_n | solution.py:65
  209.7 10.3 %bitcast_reduce_fusion = (f32[3,4,128]{2,1,0:T(4,128)S(1)}, bf16[3,4,2048,128]{3,2,1,0:T(8,128)(2,1)}) fusion(pred[4,2048]{1,0:T(4,128)(4,1)S(1)} %bitcast.72, bf16[3,4,2048,128]{3,2,1,0:T(8,128)(2,1)} %bitcast.54, bf16[3,4,128,128]{3,2,1,0:T(8,128)(2,1)S(1)} %bitcast.66), kind=kOutput, calls=%fused_computation.3 | convolution fusion | flops 1632634880 | bytes 12990464 | tf_op jit(solution)/shard_map/sub | solution.py:25
  220.0 6.6 %fusion.10 = bf16[3,4,128,128]{3,2,1,0:T(8,128)(2,1)S(1)} fusion(bf16[3,4,2048,128]{3,2,1,0:T(8,128)(2,1)} %bitcast.55, f32[3,4,128]{2,1,0:T(4,128)S(1)} %get-tuple-element.8, bf16[3,4,2048,128]{3,2,1,0:T(8,128)(2,1)} %get-tuple-element.9), kind=kOutput, calls=%fused_computation.17 | convolution fusion | flops 805699584 | bytes 12982272 | tf_op jit(solution)/shard_map/hbqk,hbkd->hbqd/dot_general | solution.py:27
  226.7 0.2 copy.34
  226.9 3.5 %convolution_convert_fusion = bf16[512,3072]{1,0:T(8,128)(2,1)} fusion(bf16[512,384]{0,1:T(8,128)(2,1)S(1)} %bitcast.71, bf16[384,3072]{1,0:T(8,128)(2,1)S(1)} %copy-done), kind=kOutput, calls=%fused_computation.15 | convolution fusion | flops 1209532416 | bytes 5898240 | tf_op jit(solution)/shard_map/dot_general | solution.py:76
  230.4 85.2 %reduce-scatter.2.cloned.1.call-done = bf16[64,3072]{1,0:T(8,128)(2,1)} async-done(((bf16[512,3072]{1,0:T(8,128)(2,1)}), bf16[64,3072]{1,0:T(8,128)(2,1)}) %reduce-scatter.2.cloned.1.call-update) | async-done | bytes 393232 | tf_op jit(solution)/shard_map/reduce_scatter | solution.py:75
  (19 shorter events, 0.4 us)
Async XLA Ops:
  6.5 220.3 %copy-start = (bf16[384,3072]{1,0:T(8,128)(2,1)S(1)}, bf16[384,3072]{1,0:T(8,128)(2,1)}, u32[]{:S(2)}) copy-start(bf16[384,3072]{1,0:T(8,128)(2,1)} %param.10) | copy-start | bytes 7077892
  6.5 38.5 %copy-start.1 = (s32[4,16]{1,0:T(4,128)S(1)}, s32[4,16]{1,0:T(4,128)}, u32[]{:S(2)}) copy-start(s32[4,16]{1,0:T(4,128)} %param.11) | copy-start | bytes 772
  6.5 99.5 %all-gather.3.cloned.1.call-start = ((), (), s32[]{:S(2)}) async-start(), calls=%async_computation.4 | async-start | bytes 12976128 | tf_op jit(solution)/shard_map/all_gather | solution.py:55
  25.6 162.0 %all-gather.5.cloned.1.call-start = ((), (), s32[]{:S(2)}) async-start(), calls=%async_computation.5 | async-start | bytes 12976128 | tf_op jit(solution)/shard_map/all_gather | solution.py:56
  41.5 12.6 %all-to-all-start.1 = ((bf16[64,8,384]{2,0,1:T(8,128)(2,1)}), bf16[64,8,384]{2,0,1:T(8,128)(2,1)S(1)}, u32[]{:S(2)}, u32[]{:S(2)}) async-start(bf16[64,8,384]{2,0,1:T(8,128)(2,1)} %bitcast.51), calls=%async_computation.1 | async-start | bytes 786432 | tf_op jit(solution)/shard_map/all_to_all | solution.py:38
  45.0 270.6 %reduce-scatter.2.cloned.1.call-start = ((), (), s32[]{:S(2)}) async-start(), calls=%async_computation.6 | async-start | bytes 3538944 | tf_op jit(solution)/shard_map/reduce_scatter | solution.py:75
Sparse Core Ops, SparseCore 0:
  25.7 80.2 all-gather.2
  107.9 79.6 all-gather.4
  230.5 85.0 reduce-scatter.1
where the time goes:
time: 323 us; the launch traced here: 322 us
  waiting for transfers between devices  219 us (68%)
  local copies, waits for them, and re-layouts  31.7 us (10%)
  blocking collectives  28.9 us (9%)
  matrix products  20.4 us (6%)
  between operations  13.2 us (4%)
  other arithmetic  5.58 us (2%)
  starting transfers between devices  3.54 us (1%)
    reduce_scatter x1, waiting for transfers between devices, on_device(): lax.psum_scatter(jnp.dot(attended, out_weight, preferred_element_type=jnp...  85.2 us
    all_gather x1, waiting for transfers between devices, on_device(): lax.all_gather(value_heads, 'blk', axis=1, tiled=True)  72.9 us
    all_gather x1, waiting for transfers between devices, on_device(): lax.all_gather(key_heads, 'blk', axis=1, tiled=True)  51.7 us
    all_to_all x1, blocking collectives, on_device(): lax.all_to_all(key_tokens, 'head', split_axis=1, concat_axis=0, tiled=True)  16.9 us
    all_to_all x1, blocking collectives, on_device(): lax.all_to_all(value_tokens, 'head', split_axis=1, concat_axis=0, tiled=T...  12 us
    sub x1, matrix products, sparse_attend(): weights = jnp.where(mask_full, jnp.exp(scores - peak_value), 0.0)  10.3 us
    all_to_all x1, waiting for transfers between devices, on_device(): lax.all_to_all(query_tokens, 'head', split_axis=1, concat_axis=0, tiled=T...  8.89 us
    gather x1, local copies, waits for them, and re-layouts, on_device(): jnp.take(source_keys, flat_index, axis=1)  8.63 us
  transfers between devices with their start and end apart: 4, of which 4 were waited for; matrix products, arithmetic and copies ran while one was open for 4% of the time, Pallas kernels for 0%

commit v1 on v0

--- a/solution.py
+++ b/solution.py
@@ -1,3 +1,4 @@
+import functools
 import math
 import jax
 import jax.numpy as jnp
@@ -6,6 +7,18 @@
 
 HD = 128
 masked_low = -1e30
+
+
+def plan_ends(sample, device_axis):
+    chunks = []
+    for _ in range(lax.axis_size(device_axis)):
+        chunks.append(sample)
+    passed = jnp.stack(chunks, axis=0)
+    carry_in = lax.all_to_all(passed, device_axis, split_axis=0, concat_axis=0)
+    return jnp.concatenate(carry_in, axis=1)
+
+
+derive_masks = functools.partial(plan_ends, device_axis="blk")
 
 
 def sparse_attend(query_sets, key_sets, value_sets, present):
@@ -52,7 +65,7 @@
     present = kv_blocks >= 0
     safe_index = jnp.maximum(kv_blocks, 0)
     gathered_keys, gathered_values = (
-        lax.all_gather(key_heads, "blk", axis=1, tiled=True),
+        derive_masks(key_heads),
         lax.all_gather(value_heads, "blk", axis=1, tiled=True),
     )
     total_blocks = gathered_keys.shape[1] // block_rows

time: 323 us -> 558 us (1.73)
  waiting for transfers between devices: 219 us -> 442 us
  blocking collectives: 28.9 us -> 0 us
  starting transfers between devices: 3.54 us -> 23.7 us
  local copies, waits for them, and re-layouts: 31.7 us -> 51.8 us
    all_to_all x0 -> x3, waiting for transfers between devices: none -> 345 us  [the longest x1 329 us: plan_ends(): carry_in = lax.all_to_all(passed, device_axis, split_axis=0, concat_axis=0)]
    all_gather x1, waiting for transfers between devices: 72.9 us -> 0.01 us  [on_device(): lax.all_gather(value_heads, 'blk', axis=1, tiled=True)]
    all_gather x1 -> x0, waiting for transfers between devices: 51.7 us -> none  [on_device(): lax.all_gather(key_heads, 'blk', axis=1, tiled=True)]
    all_to_all x2 -> x0, blocking collectives: 28.9 us -> none  [the longest x1 16.9 us: on_device(): lax.all_to_all(key_tokens, 'head', split_axis=1, concat_axis=0, tiled=True)]
    all_to_all x0 -> x3, starting transfers between devices: none -> 19.3 us  [the longest x1 8.94 us: plan_ends(): carry_in = lax.all_to_all(passed, device_axis, split_axis=0, concat_axis=0)]
    all_to_all x0 -> x1, local copies, waits for them, and re-layouts: none -> 10.7 us  [plan_ends(): carry_in = lax.all_to_all(passed, device_axis, split_axis=0, concat_axis=0)]
    another operation x0 -> x1, local copies, waits for them, and re-layouts: none -> 7.7 us  [plan_ends(): passed = jnp.stack(chunks, axis=0)]
  transfers between devices with their start and end apart: 4 -> 6, of which waited for: 4 -> 5; matrix products, arithmetic and copies ran while one was open for 4% -> 5% of each run, Pallas kernels for 0% -> 0%
where the time goes in v1:
time: 558 us; the launch traced here: 557 us
  waiting for transfers between devices  442 us (79%)
  local copies, waits for them, and re-layouts  51.8 us (9%)
  starting transfers between devices  23.7 us (4%)
  matrix products  20.4 us (4%)
  between operations  13.6 us (2%)
  other arithmetic  5.58 us (1%)
    all_to_all x1, waiting for transfers between devices, plan_ends(): carry_in = lax.all_to_all(passed, device_axis, split_axis=0, concat_axis=0)  329 us
    reduce_scatter x1, waiting for transfers between devices, on_device(): lax.psum_scatter(jnp.dot(attended, out_weight, preferred_element_type=jnp...  88.8 us
  transfers between devices with their start and end apart: 6, of which 5 were waited for; matrix products, arithmetic and copies ran while one was open for 5% of the time, Pallas kernels for 0%

profile of v1, /device:TPU:32, one launch (start us, length us, event | category | flops | bytes accessed | tf_op | source)
XLA Modules:
  0.0 557.4 jit_solution(7965119695236095440)
XLA Ops:
  6.5 1.9 copy.48
  8.5 6.9 %all-to-all-start = ((bf16[64,8,384]{2,0,1:T(8,128)(2,1)}), bf16[64,8,384]{2,0,1:T(8,128)(2,1)S(1)}, u32[]{:S(2)}, u32[]{:S(2)}) async-start(bf16[64,8,384]{2,0,1:T(8,128)(2,1)} %bitcast.54), calls=%async_computation | async-start | bytes 786432 | tf_op jit(solution)/shard_map/all_to_all | solution.py:52
  15.4 1.8 copy.46
  17.2 8.2 %all-to-all-done = bf16[64,8,384]{2,0,1:T(8,128)(2,1)S(1)} async-done(((bf16[64,8,384]{2,0,1:T(8,128)(2,1)}), bf16[64,8,384]{2,0,1:T(8,128)(2,1)S(1)}, u32[]{:S(2)}, u32[]{:S(2)}) %all-to-all-start) | async-done | bytes 393248 | tf_op jit(solution)/shard_map/all_to_all | solution.py:52
  25.4 3.5 all-to-all-start.3
  28.8 1.8 copy.47
  30.6 7.6 %all-to-all-done.3 = bf16[64,8,384]{2,0,1:T(8,128)(2,1)S(1)} async-done(((bf16[64,8,384]{2,0,1:T(8,128)(2,1)}), bf16[64,8,384]{2,0,1:T(8,128)(2,1)S(1)}, u32[]{:S(2)}, u32[]{:S(2)}) %all-to-all-start.3) | async-done | bytes 393248 | tf_op jit(solution)/shard_map/all_to_all | solution.py:53
  38.2 4.1 all-to-all-start.2
  42.5 9.1 %all-to-all-done.2 = bf16[64,8,384]{2,0,1:T(8,128)(2,1)} async-done(((bf16[64,8,384]{2,0,1:T(8,128)(2,1)}), bf16[64,8,384]{2,0,1:T(8,128)(2,1)}, u32[]{:S(2)}, u32[]{:S(2)}) %all-to-all-start.2) | async-done | bytes 393248 | tf_op jit(solution)/shard_map/all_to_all | solution.py:51
  51.6 7.7 %stack.2 = bf16[32,3,512,128]{3,2,1,0:T(8,128)(2,1)} broadcast(bf16[3,512,128]{2,1,0:T(8,128)(2,1)S(1)} %copy.27), dimensions={1,2,3} | broadcast | bytes 12976128 | tf_op jit(solution)/shard_map/stack | solution.py:16
  59.3 8.9 %all-to-all-start.1 = ((bf16[32,3,512,128]{3,2,1,0:T(8,128)(2,1)}), bf16[32,3,512,128]{3,2,1,0:T(8,128)(2,1)}, u32[]{:S(2)}, u32[]{:S(2)}) async-start(bf16[32,3,512,128]{3,2,1,0:T(8,128)(2,1)} %stack.2), calls=%async_computation.1 | async-start | bytes 25165824 | tf_op jit(solution)/shard_map/all_to_all | solution.py:17
  68.4 0.8 copy.33
  69.7 1.4 reshape.58
  71.2 328.8 %all-to-all-done.1 = bf16[32,3,512,128]{3,2,1,0:T(8,128)(2,1)} async-done(((bf16[32,3,512,128]{3,2,1,0:T(8,128)(2,1)}), bf16[32,3,512,128]{3,2,1,0:T(8,128)(2,1)}, u32[]{:S(2)}, u32[]{:S(2)}) %all-to-all-start.1) | async-done | bytes 12582944 | tf_op jit(solution)/shard_map/all_to_all | solution.py:17
  399.9 10.7 %copy.28 = bf16[32,3,512,128]{3,2,0,1:T(8,128)(2,1)} copy(bf16[32,3,512,128]{3,2,1,0:T(8,128)(2,1)} %all-to-all-done.1) | data formatting | bytes 25165824 | tf_op jit(solution)/shard_map/all_to_all | solution.py:17
  410.6 8.5 %gather_fusion = bf16[64,3,128,128]{3,2,1,0:T(8,128)(2,1)} fusion(bf16[3,128,128,128]{3,2,1,0:T(8,128)(2,1)} %bitcast.56, s32[1024]{0:T(1024)S(1)} %pad_clamp_fusion), kind=kCustom, calls=%fused_computation.clone | custom fusion | bytes 12583168 | tf_op jit(solution)/shard_map/jit(_take)/gather | solution.py:75
  419.1 8.5 %gather_fusion.1 = bf16[64,3,128,128]{3,2,1,0:T(8,128)(2,1)} fusion(bf16[3,128,128,128]{3,2,1,0:T(8,128)(2,1)} %bitcast.59, s32[1024]{0:T(1024)S(1)} %pad_clamp_fusion), kind=kCustom, calls=%fused_computation.1.clone | custom fusion | bytes 12583168 | tf_op jit(solution)/shard_map/jit(_take)/gather | solution.py:78
  427.6 5.5 select_bitcast_fusion.1
  433.2 4.0 copy.34
  437.2 4.0 copy.29
  441.2 10.3 %bitcast_reduce_fusion = (f32[3,4,128]{2,1,0:T(4,128)S(1)}, bf16[3,4,2048,128]{3,2,1,0:T(8,128)(2,1)}) fusion(pred[4,2048]{1,0:T(4,128)(4,1)S(1)} %bitcast.73, bf16[3,4,2048,128]{3,2,1,0:T(8,128)(2,1)} %bitcast.58, bf16[3,4,128,128]{3,2,1,0:T(8,128)(2,1)S(1)} %bitcast.67), kind=kOutput, calls=%fused_computation.3 | convolution fusion | flops 1632634880 | bytes 12990464 | tf_op jit(solution)/shard_map/sub | solution.py:38
  451.5 6.6 %fusion.10 = bf16[3,4,128,128]{3,2,1,0:T(8,128)(2,1)S(1)} fusion(bf16[3,4,2048,128]{3,2,1,0:T(8,128)(2,1)} %bitcast.57, f32[3,4,128]{2,1,0:T(4,128)S(1)} %get-tuple-element.8, bf16[3,4,2048,128]{3,2,1,0:T(8,128)(2,1)} %get-tuple-element.9), kind=kOutput, calls=%fused_computation.17 | convolution fusion | flops 805699584 | bytes 12982272 | tf_op jit(solution)/shard_map/hbqk,hbkd->hbqd/dot_general | solution.py:40
  458.3 3.5 convolution_convert_fusion
  461.8 88.8 %reduce-scatter.2.cloned.1.call-done = bf16[64,3072]{1,0:T(8,128)(2,1)} async-done(((bf16[512,3072]{1,0:T(8,128)(2,1)}), bf16[64,3072]{1,0:T(8,128)(2,1)}) %reduce-scatter.2.cloned.1.call-update) | async-done | bytes 393232 | tf_op jit(solution)/shard_map/reduce_scatter | solution.py:88
  (26 shorter events, 1.0 us)
Async XLA Ops:
  6.5 451.8 %copy-start = (bf16[384,3072]{1,0:T(8,128)(2,1)S(1)}, bf16[384,3072]{1,0:T(8,128)(2,1)}, u32[]{:S(2)}) copy-start(bf16[384,3072]{1,0:T(8,128)(2,1)} %param.10) | copy-start | bytes 7077892
  8.5 16.9 %all-to-all-start = ((bf16[64,8,384]{2,0,1:T(8,128)(2,1)}), bf16[64,8,384]{2,0,1:T(8,128)(2,1)S(1)}, u32[]{:S(2)}, u32[]{:S(2)}) async-start(bf16[64,8,384]{2,0,1:T(8,128)(2,1)} %bitcast.54), calls=%async_computation | async-start | bytes 786432 | tf_op jit(solution)/shard_map/all_to_all | solution.py:52
  25.4 12.8 %all-to-all-start.3 = ((bf16[64,8,384]{2,0,1:T(8,128)(2,1)}), bf16[64,8,384]{2,0,1:T(8,128)(2,1)S(1)}, u32[]{:S(2)}, u32[]{:S(2)}) async-start(bf16[64,8,384]{2,0,1:T(8,128)(2,1)} %bitcast.66), calls=%async_computation.3 | async-start | bytes 786432 | tf_op jit(solution)/shard_map/all_to_all | solution.py:53
  38.2 4.1 copy-start.1
  38.2 13.4 %all-to-all-start.2 = ((bf16[64,8,384]{2,0,1:T(8,128)(2,1)}), bf16[64,8,384]{2,0,1:T(8,128)(2,1)}, u32[]{:S(2)}, u32[]{:S(2)}) async-start(bf16[64,8,384]{2,0,1:T(8,128)(2,1)} %bitcast.65), calls=%async_computation.2 | async-start | bytes 786432 | tf_op jit(solution)/shard_map/all_to_all | solution.py:51
  59.3 9.0 %copy-start.2 = (bf16[64,8,384]{2,0,1:T(8,128)(2,1)S(1)}, bf16[64,8,384]{2,0,1:T(8,128)(2,1)}, u32[]{:S(2)}) copy-start(bf16[64,8,384]{2,0,1:T(8,128)(2,1)} %copy-done.1) | copy-start | bytes 1179652
  59.3 10.2 %copy-start.3 = (s32[4,16]{1,0:T(4,128)S(1)}, s32[4,16]{1,0:T(4,128)}, u32[]{:S(2)}) copy-start(s32[4,16]{1,0:T(4,128)} %param.11) | copy-start | bytes 772
  59.3 340.7 %all-to-all-start.1 = ((bf16[32,3,512,128]{3,2,1,0:T(8,128)(2,1)}), bf16[32,3,512,128]{3,2,1,0:T(8,128)(2,1)}, u32[]{:S(2)}, u32[]{:S(2)}) async-start(bf16[32,3,512,128]{3,2,1,0:T(8,128)(2,1)} %stack.2), calls=%async_computation.1 | async-start | bytes 25165824 | tf_op jit(solution)/shard_map/all_to_all | solution.py:17
  68.2 350.9 %all-gather.2.cloned.1.call-start = ((), (), s32[]{:S(2)}) async-start(), calls=%async_computation.5 | async-start | bytes 12976128 | tf_op jit(solution)/shard_map/all_gather | solution.py:69
  69.2 481.4 %reduce-scatter.2.cloned.1.call-start = ((), (), s32[]{:S(2)}) async-start(), calls=%async_computation.6 | async-start | bytes 3538944 | tf_op jit(solution)/shard_map/reduce_scatter | solution.py:88
Sparse Core Ops, SparseCore 0:
  70.9 272.6 all-gather.1
  461.9 88.6 reduce-scatter.1
